TPU v7x, 128 devices: a whole 4x4x4 slice. The times are simulated.
128 devices in a mesh: gx: 32 (over y, z, x_hi), gy: 4 (over x_lo, core).
Axes of the slice: x: 4 (x_hi: 2, x_lo: 2; x = x_hi * 2 + x_lo), y: 4, z: 4, core: 2. Of those that a mesh axis runs over, the one named last changes fastest.
Arguments:
- density: bfloat16 [32, 4, 3, 20, 128, 128], P('gx', 'gy'), may hold values from -0.3 to 0.8
- neighbours: int32 [32, 4, 3, 20], replicated, may hold values from 0 to 383, as said below
- ent_blocks: bfloat16 [12288, 128, 128], P(('gx', 'gy')), may hold values from -0.59765625 to 0.59765625
- ent_owner: int32 [12288], replicated, may hold values from 0 to 127, as said below
- ent_place: int32 [12288], replicated, may hold values from 0 to 59
Outputs:
- purified: float32 [32, 4, 3, 20, 128, 128], P('gx', 'gy')
Inputs may be any that keep to these rules, and one draw needn't show every extreme that they name: neighbours[x, y, r, 0] is the row's own index (x * 4 + y) * 3 + r; the other 19 entries of a row are distinct rows of devices (x + a mod 32, y + b mod 4) with a and b in -1, 0, 1. `ent_owner`: among the 96 entries d * 96 to d * 96 + 95 of one device d, no owner is named more than 2 times, and some owner exactly 2 times.
All inputs are finite; a program needn't handle non-finite values.
Results may differ from a plain program's by a relative error of at most 0.0059.
Values may be sent and summed in bfloat16 or wider, within the bound.
No kernel may reach another device: no remote copies, remote signals or barrier semaphores. Data moves between devices by JAX's collectives and lax.ppermute only.
A program may use at most 128 MiB of HBM per device.

v0:
```python
import functools

import jax
import jax.numpy as jnp
from jax import lax
from jax.experimental import pallas as pl
from jax.experimental.pallas import tpu as pltpu
from jax.sharding import PartitionSpec as P

C = 2


def pack_kernel(slots_ref, ent_ref, out_ref, staged, load_sems, store_sem):
    count = ent_ref.shape[0]
    parts = load_sems.shape[0]
    size = count // parts
    loads = []
    for p in range(parts):
        rows = pl.ds(p * size, size)
        loads.append(pltpu.make_async_copy(ent_ref.at[rows], staged.at[rows], load_sems.at[p]))
        loads[-1].start()

    def issue(i, carry):
        pltpu.make_async_copy(staged.at[i], out_ref.at[slots_ref[i]], store_sem).start()
        return carry

    for p in range(parts):
        loads[p].wait()
        lax.fori_loop(p * size, (p + 1) * size, issue, 0)
    pltpu.make_async_copy(staged, out_ref.at[pl.ds(0, count)], store_sem).wait()


def pack(ent_blocks, slots, total):
    return pl.pallas_call(
        pack_kernel,
        out_shape=jax.ShapeDtypeStruct((total,) + ent_blocks.shape[1:], ent_blocks.dtype),
        in_specs=[
            pl.BlockSpec(memory_space=pltpu.SMEM),
            pl.BlockSpec(memory_space=pl.ANY),
        ],
        out_specs=pl.BlockSpec(memory_space=pl.ANY),
        scratch_shapes=[
            pltpu.VMEM(ent_blocks.shape, ent_blocks.dtype),
            pltpu.SemaphoreType.DMA((4,)),
            pltpu.SemaphoreType.DMA,
        ],
        name="pack",
    )(slots, ent_blocks)


def admit_kernel(first_ref, order_ref, stored_ref, density_ref, received_ref, out_ref):
    def target(t, carry):
        def add(j, total):
            return total + received_ref[order_ref[j]].astype(jnp.float32)

        total = lax.fori_loop(
            first_ref[t], first_ref[t + 1], add, density_ref[t].astype(jnp.float32)
        )
        out_ref[stored_ref[t]] = total.astype(out_ref.dtype)
        return carry

    lax.fori_loop(0, density_ref.shape[0], target, 0)


def admit(density, received, first, order, stored):
    return pl.pallas_call(
        admit_kernel,
        out_shape=jax.ShapeDtypeStruct(density.shape, density.dtype),
        in_specs=[
            pl.BlockSpec(memory_space=pltpu.SMEM),
            pl.BlockSpec(memory_space=pltpu.SMEM),
            pl.BlockSpec(memory_space=pltpu.SMEM),
            pl.BlockSpec(memory_space=pltpu.VMEM),
            pl.BlockSpec(memory_space=pltpu.VMEM),
        ],
        out_specs=pl.BlockSpec(memory_space=pltpu.VMEM),
        name="admit",
    )(first, order, stored, density, received)


def purify_kernel(row_count, slot_count, width, piece_starts, zero_at, pos_ref, stored_ref, *refs):
    pieces = refs[: len(piece_starts)]
    out_ref, table, left, gathered, square, square_b, sems = refs[len(piece_starts):]
    pair = 2 * width
    copies = []
    for i, (piece, start) in enumerate(zip(pieces, piece_starts)):
        copy = pltpu.make_async_copy(piece, table.at[pl.ds(start, piece.shape[0])], sems.at[i])
        copy.start()
        copies.append(copy)
    table[zero_at] = jnp.zeros((width, width), table.dtype)
    for copy in copies:
        copy.wait()

    def row(r, carry):
        base = r * slot_count * slot_count
        for m in range(slot_count):
            left[:, m * width:(m + 1) * width] = table[stored_ref[r * slot_count + m]]
        for k in range(0, slot_count, 2):
            for m in range(slot_count):
                for j in range(2):
                    gathered[
                        m * width:(m + 1) * width, (k + j) * width:(k + j + 1) * width
                    ] = table[pos_ref[base + m * slot_count + k + j]]
            lanes = slice(k * width, k * width + pair)
            product = jnp.dot(
                left[...], gathered[:, lanes], preferred_element_type=jnp.float32
            )
            square[:, lanes] = product
            square_b[:, lanes] = product.astype(jnp.bfloat16)
        for k in range(0, slot_count, 2):
            lanes = slice(k * width, k * width + pair)
            product = jnp.dot(
                square_b[...], gathered[:, lanes], preferred_element_type=jnp.float32
            )
            result = 3.0 * square[:, lanes] - 2.0 * product
            out_ref[r * slot_count + k] = result[:, :width]
            out_ref[r * slot_count + k + 1] = result[:, width:]
        return carry

    lax.fori_loop(0, row_count, row, 0)


def purify(positions, stored, pieces, piece_starts, zero_at, row_count, slot_count, width):
    span = slot_count * width
    return pl.pallas_call(
        functools.partial(purify_kernel, row_count, slot_count, width, piece_starts, zero_at),
        out_shape=jax.ShapeDtypeStruct((row_count * slot_count, width, width), jnp.float32),
        in_specs=[pl.BlockSpec(memory_space=pltpu.SMEM)] * 2
        + [pl.BlockSpec(memory_space=pl.ANY)] * len(pieces),
        out_specs=pl.BlockSpec(memory_space=pltpu.VMEM),
        scratch_shapes=[
            pltpu.VMEM((zero_at + 1, width, width), jnp.bfloat16),
            pltpu.VMEM((width, span), jnp.bfloat16),
            pltpu.VMEM((span, span), jnp.bfloat16),
            pltpu.VMEM((width, span), jnp.float32),
            pltpu.VMEM((width, span), jnp.bfloat16),
            pltpu.SemaphoreType.DMA((len(pieces),)),
        ],
        name="purify",
    )(positions, stored, *pieces)


def block_positions(neighbours, here_x, here_y, my_columns, starts, zero_at):
    wide_count, narrow_count, row_count, slot_count = neighbours.shape
    listing = neighbours.reshape(wide_count * narrow_count * row_count, slot_count)
    inner_lists = jnp.take(listing, my_columns, axis=0)
    inner_x = my_columns // (narrow_count * row_count)
    inner_y = my_columns // row_count % narrow_count
    inner_r = my_columns % row_count
    list_x = inner_lists // (narrow_count * row_count)
    list_y = inner_lists // row_count % narrow_count
    kind = jnp.where(
        list_x == (inner_x ^ 1)[:, :, None], 2, jnp.where(list_y == (inner_y ^ 1)[:, :, None], 1, 0)
    )
    slot_ids = jnp.arange(slot_count, dtype=jnp.int32)
    key = kind * slot_count + slot_ids
    place = jnp.sum((key[:, :, :, None] > key[:, :, None, :]).astype(jnp.int32), axis=3)
    matches = inner_lists[:, :, None, :] == my_columns[:, None, :, None]
    present = jnp.any(matches, axis=3)
    inner_place = jnp.sum(jnp.where(matches, place[:, :, None, :], 0), axis=3)
    near_x = jnp.where(inner_x == here_x, 0, jnp.where(inner_x == here_x ^ 1, 1, 2))
    near_y = jnp.where(inner_y == here_y, 0, jnp.where(inner_y == here_y ^ 1, 1, 2))
    near = near_x * 3 + near_y
    near_start = jnp.zeros_like(near)
    for i, start in enumerate(starts):
        near_start = jnp.where(near == i, start, near_start)
    position = (near_start + inner_r)[:, :, None] + inner_place * row_count
    positions = jnp.where(present, position, zero_at).astype(jnp.int32)
    own_places = place[:, 0] * row_count + jnp.arange(row_count, dtype=jnp.int32)[:, None]
    return positions.reshape(-1), own_places.astype(jnp.int32).reshape(-1)


def per_device(density, neighbours, ent_blocks, ent_owner, ent_place):
    wide_count = lax.axis_size("gx")
    narrow_count = lax.axis_size("gy")
    device_count = wide_count * narrow_count
    here_x = lax.axis_index("gx")
    here_y = lax.axis_index("gy")
    self_index = here_x * narrow_count + here_y
    row_count = density.shape[2]
    slot_count = density.shape[3]
    width = density.shape[4]
    blocks = row_count * slot_count
    held = ent_blocks.shape[0]
    owners = ent_owner.reshape(device_count, held)
    places = ent_place.reshape(device_count, held)

    my_owners = lax.dynamic_index_in_dim(owners, self_index, 0, False)
    entry_ids = jnp.arange(held, dtype=jnp.int32)
    same = my_owners[:, None] == my_owners[None, :]
    my_ranks = jnp.sum(same & (entry_ids[None, :] < entry_ids[:, None]), axis=1)
    slots = (my_owners * C + my_ranks).astype(jnp.int32)
    outgoing = pack(ent_blocks, slots, device_count * C)
    received = lax.all_to_all(
        outgoing.reshape(device_count, C, width, width),
        ("gx", "gy"), split_axis=0, concat_axis=0, tiled=True,
    ).reshape(device_count * C, width, width)

    for_me = (owners == self_index).astype(jnp.int32)
    rank = jnp.cumsum(for_me, axis=1) - for_me
    picked = (for_me[:, :, None] == 1) & (
        rank[:, :, None] == jnp.arange(C, dtype=jnp.int32)[None, None, :]
    )
    slot_place = jnp.sum(jnp.where(picked, places[:, :, None], 0), axis=1).reshape(-1)
    slot_used = jnp.any(picked, axis=1).reshape(-1)
    slot_place = jnp.where(slot_used, slot_place, blocks)
    slot_ids = jnp.arange(device_count * C, dtype=jnp.int32)
    ahead = (slot_place[:, None] > slot_place[None, :]) | (
        (slot_place[:, None] == slot_place[None, :]) & (slot_ids[:, None] > slot_ids[None, :])
    )
    sorted_at = jnp.sum(ahead, axis=1)
    order = jnp.sum(
        jnp.where(sorted_at[None, :] == slot_ids[:, None], slot_ids[None, :], 0), axis=1
    ).astype(jnp.int32)
    target_ids = jnp.arange(blocks + 1, dtype=jnp.int32)
    first = jnp.sum(slot_place[None, :] < target_ids[:, None], axis=1).astype(jnp.int32)

    near_blocks = row_count * min(slot_count, 6 * row_count)
    corner_blocks = row_count * min(slot_count, 4 * row_count)
    sizes = [blocks] * 6 + [near_blocks, near_blocks, corner_blocks]
    starts = [sum(sizes[:i]) for i in range(9)]
    zero_at = sum(sizes)
    my_columns = lax.dynamic_index_in_dim(
        lax.dynamic_index_in_dim(neighbours, here_x, 0, False), here_y, 0, False
    )
    positions, stored = block_positions(neighbours, here_x, here_y, my_columns, starts, zero_at)

    own = admit(density.reshape(blocks, width, width), received, first, order, stored)

    axes = ("gx", "gy")
    devices = [(x, y) for x in range(wide_count) for y in range(narrow_count)]

    def send(array, target):
        pairs = []
        for x, y in devices:
            to_x, to_y = target(x, y)
            pairs.append((x * narrow_count + y, to_x % wide_count * narrow_count + to_y))
        return lax.ppermute(array, axes, pairs)

    def across(x, y):
        return x, narrow_count - 1 - y

    def chip(x, y):
        return x, y ^ 1

    def ring(x, y):
        return x ^ 1, narrow_count - 1 - y

    def onward(x, y):
        return (x + 2 if x % 2 == 0 else x - 2), y

    half = blocks // 2
    ring_across_a = send(own[:half], ring)
    own_across_b = send(own[half:], across)
    own_chip = send(own, chip)
    ring_same_a = send(ring_across_a, across)
    far_across_a = send(ring_across_a, onward)
    ring_same_b = send(own_across_b, ring)
    ring_across_b = send(own[half:], ring)
    own_across_a = send(own[:half], across)
    far_same_a = send(ring_same_a, onward)
    ring_chip_a = send(ring_same_a, chip)
    far_same_b = send(ring_same_b[:near_blocks - half], onward)
    ring_chip_b = send(ring_same_b, chip)
    far_across_b = send(ring_across_b[:corner_blocks - half], onward)
    far_chip_a = send(far_same_a, chip)
    far_chip_b = send(far_same_b, chip)

    pieces = [
        (own, 0, 0), (own_chip, 1, 0), (own_across_a, 2, 0), (own_across_b, 2, half),
        (ring_same_a, 3, 0), (ring_same_b, 3, half), (ring_chip_a, 4, 0), (ring_chip_b, 4, half),
        (ring_across_a, 5, 0), (ring_across_b, 5, half),
        (far_same_a, 6, 0), (far_same_b, 6, half), (far_chip_a, 7, 0), (far_chip_b, 7, half),
        (far_across_a, 8, 0), (far_across_b, 8, half),
    ]
    purified = purify(
        positions, stored, [piece for piece, _, _ in pieces],
        [starts[part] + offset for _, part, offset in pieces],
        zero_at, row_count, slot_count, width,
    )
    return purified.reshape(density.shape)


def solution(mesh):
    in_specs = (P("gx", "gy", None, None, None, None), P(), P(("gx", "gy"), None, None), P(), P())
    out_specs = P("gx", "gy", None, None, None, None)
    return jax.shard_map(
        per_device, mesh=mesh, in_specs=in_specs, out_specs=out_specs, check_vma=False
    )
```

profile of v0, /device:TPU:1, one launch (start us, length us, event | category | flops | bytes accessed | tf_op | source)
XLA Modules:
  0.0 279.6 jit_solution(11841560607700934229)
XLA Ops:
  0.0 0.9 reshape.283
  1.1 0.5 multiply_add_fusion.slots_ref
  1.6 3.5 %pack.1 = bf16[256,128,128]{2,1,0:T(8,128)(2,1)} custom-call(s32[96]{0:T(128)} %multiply_add_fusion.slots_ref, bf16[96,128,128]{2,1,0:T(8,128)(2,1)} %ent_ref.1), custom_call_target="tpu_custom_call" | custom-call | tf_op jit(solution)/shard_map/pack/pallas_call | solution.py:34
  5.1 12.0 %all-to-all-start = ((bf16[128,2,128,128]{3,2,1,0:T(8,128)(2,1)}), bf16[128,2,128,128]{3,2,1,0:T(8,128)(2,1)}, u32[]{:S(2)}, u32[]{:S(2)}) async-start(bf16[128,2,128,128]{3,2,1,0:T(8,128)(2,1)} %bitcast.8), calls=%async_computation | async-start | bytes 16777216 | tf_op jit(solution)/shard_map/all_to_all | solution.py:194
  17.4 1.2 dynamic-slice_reduce_fusion
  19.7 0.6 gather_fusion
  20.5 1.3 convert_reduce_fusion
  21.9 0.5 add.180.stored_ref
  22.4 0.6 convert_reduce_fusion.2.first_ref
  23.2 0.7 select_reduce_fusion.order_ref
  23.9 92.6 %all-to-all-done = bf16[128,2,128,128]{3,2,1,0:T(8,128)(2,1)} async-done(((bf16[128,2,128,128]{3,2,1,0:T(8,128)(2,1)}), bf16[128,2,128,128]{3,2,1,0:T(8,128)(2,1)}, u32[]{:S(2)}, u32[]{:S(2)}) %all-to-all-start) | async-done | bytes 8388640 | tf_op jit(solution)/shard_map/all_to_all | solution.py:194
  116.5 7.3 %admit.1.refs_0_ = bf16[60,128,128]{2,1,0:T(8,128)(2,1)} custom-call(s32[61]{0:T(128)} %convert_reduce_fusion.2.first_ref, s32[256]{0:T(256)} %select_reduce_fusion.order_ref, s32[60]{0:T(128)} %add.180.stored_ref, bf16[60,128,128]{2,1,0:T(8,128)(2,1)} %bitcast.9, bf16[256,128,128]{2,1,0:T(8,128)(2,1)} %bitcast.3.received_ref), custom_call_target="tpu_custom_call" | custom-call | tf_op jit(solution)/shard_map/admit/pallas_call | solution.py:66
  123.8 1.8 fusion.16
  125.5 6.1 %collective-permute-start.2 = (bf16[30,128,128]{2,1,0:T(8,128)(2,1)S(1)}, bf16[30,128,128]{2,1,0:T(8,128)(2,1)S(1)}, u32[]{:S(2)}, u32[]{:S(2)}) collective-permute-start(bf16[30,128,128]{2,1,0:T(8,128)(2,1)S(1)} %get-tuple-element.9), channel_id=1, source_target_pairs={{0,3},{1,2},{2,1},{3,0},{4,7},{5,6},{6,5},{7,4},{8,11},{9,10},{10,... | collective-permute-start | bytes 2949128 | tf_op jit(solution)/shard_map/ppermute | solution.py:238
  131.7 21.4 %collective-permute-done.2.refs_3_ = bf16[30,128,128]{2,1,0:T(8,128)(2,1)S(1)} collective-permute-done((bf16[30,128,128]{2,1,0:T(8,128)(2,1)S(1)}, bf16[30,128,128]{2,1,0:T(8,128)(2,1)S(1)}, u32[]{:S(2)}, u32[]{:S(2)}) %collective-permute-start.2) | collective-permute-done | bytes 983072 | tf_op jit(solution)/shard_map/ppermute | solution.py:238
  153.1 2.7 collective-permute-done.3.refs_8_
  155.7 2.0 collective-permute-start.8
  157.9 20.7 %collective-permute-done.5.refs_5_ = bf16[30,128,128]{2,1,0:T(8,128)(2,1)S(1)} collective-permute-done((bf16[30,128,128]{2,1,0:T(8,128)(2,1)S(1)}, bf16[30,128,128]{2,1,0:T(8,128)(2,1)S(1)}, u32[]{:S(2)}, u32[]{:S(2)}) %collective-permute-start.5) | collective-permute-done | bytes 983072 | tf_op jit(solution)/shard_map/ppermute | solution.py:238
  178.6 1.5 collective-permute-start.13
  180.1 1.4 collective-permute-start.9
  181.6 17.3 %collective-permute-done.8.refs_9_ = bf16[30,128,128]{2,1,0:T(8,128)(2,1)S(1)} collective-permute-done((bf16[30,128,128]{2,1,0:T(8,128)(2,1)S(1)}, bf16[30,128,128]{2,1,0:T(8,128)(2,1)S(1)}, u32[]{:S(2)}, u32[]{:S(2)}) %collective-permute-start.8) | collective-permute-done | bytes 983072 | tf_op jit(solution)/shard_map/ppermute | solution.py:238
  198.9 1.2 collective-permute-start.10
  200.1 1.3 collective-permute-start.14
  201.4 45.4 %collective-permute-done.14.refs_15_ = bf16[6,128,128]{2,1,0:T(8,128)(2,1)S(1)} collective-permute-done((bf16[6,128,128]{2,1,0:T(8,128)(2,1)S(1)}, bf16[6,128,128]{2,1,0:T(8,128)(2,1)S(1)}, u32[]{:S(2)}, u32[]{:S(2)}) %collective-permute-start.14) | collective-permute-done | bytes 196640 | tf_op jit(solution)/shard_map/ppermute | solution.py:238
  246.8 0.6 collective-permute-start.6
  247.4 0.4 copy-done.6
  247.8 0.5 collective-permute-start.11
  248.5 1.2 compare_reduce_fusion
  249.7 1.2 fusion
  251.0 0.7 select_n.305.pos_ref
  251.7 1.8 collective-permute-done.12.refs_13_
  253.4 26.0 %purify.1 = f32[60,128,128]{2,1,0:T(8,128)} custom-call(s32[1200]{0:T(1024)} %select_n.305.pos_ref, s32[60]{0:T(128)} %add.180.stored_ref, bf16[60,128,128]{2,1,0:T(8,128)(2,1)} %admit.1.refs_0_, bf16[60,128,128]{2,1,0:T(8,128)(2,1)} %collective-permute-done.refs_1_, bf16[30,128,128]{2,1,0:T(8,128)(2,1)} %copy-done.5, bf16[30,128,128]{2,1,0:T(8,128)(2,1)} %copy-done.3, ...), custom_call_target="tpu_custom_call" | custom-call | tf_op jit(solution)/shard_map/purify/pallas_call | solution.py:125
  (65 shorter events, 2.5 us)
Async XLA Ops:
  5.1 12.1 %copy-start.8 = (s32[32,4,3,20]{0,1,3,2:T(4,128)S(1)}, s32[32,4,3,20]{0,1,3,2:T(4,128)}, u32[]{:S(2)}) copy-start(s32[32,4,3,20]{0,1,3,2:T(4,128)} %param.6) | copy-start | bytes 92164
  5.1 13.9 %copy-start.9 = (s32[12288]{0:T(1024)S(1)}, s32[12288]{0:T(1024)}, u32[]{:S(2)}) copy-start(s32[12288]{0:T(1024)} %param.9) | copy-start | bytes 147460
  5.1 111.4 %all-to-all-start = ((bf16[128,2,128,128]{3,2,1,0:T(8,128)(2,1)}), bf16[128,2,128,128]{3,2,1,0:T(8,128)(2,1)}, u32[]{:S(2)}, u32[]{:S(2)}) async-start(bf16[128,2,128,128]{3,2,1,0:T(8,128)(2,1)} %bitcast.8), calls=%async_computation | async-start | bytes 16777216 | tf_op jit(solution)/shard_map/all_to_all | solution.py:194
  123.8 34.1 %copy-start = (bf16[60,128,128]{2,1,0:T(8,128)(2,1)S(1)}, bf16[60,128,128]{2,1,0:T(8,128)(2,1)}, u32[]{:S(2)}) copy-start(bf16[60,128,128]{2,1,0:T(8,128)(2,1)} %admit.1.refs_0_) | copy-start | bytes 5898244
  125.5 27.5 %collective-permute-start.2 = (bf16[30,128,128]{2,1,0:T(8,128)(2,1)S(1)}, bf16[30,128,128]{2,1,0:T(8,128)(2,1)S(1)}, u32[]{:S(2)}, u32[]{:S(2)}) collective-permute-start(bf16[30,128,128]{2,1,0:T(8,128)(2,1)S(1)} %get-tuple-element.9), channel_id=1, source_target_pairs={{0,3},{1,2},{2,1},{3,0},{4,7},{5,6},{6,5},{7,4},{8,11},{9,10},{10,... | collective-permute-start | bytes 2949128 | tf_op jit(solution)/shard_map/ppermute | solution.py:238
  131.7 24.0 %collective-permute-start.3 = (bf16[30,128,128]{2,1,0:T(8,128)(2,1)S(1)}, bf16[30,128,128]{2,1,0:T(8,128)(2,1)S(1)}, u32[]{:S(2)}, u32[]{:S(2)}) collective-permute-start(bf16[30,128,128]{2,1,0:T(8,128)(2,1)S(1)} %get-tuple-element.10), channel_id=1, source_target_pairs={{0,7},{1,6},{2,5},{3,4},{4,3},{5,2},{6,1},{7,0},{8,15},{9,14},{10,... | collective-permute-start | bytes 2949128 | tf_op jit(solution)/shard_map/ppermute | solution.py:238
  153.1 25.6 %copy-start.3 = (bf16[30,128,128]{2,1,0:T(8,128)(2,1)}, bf16[30,128,128]{2,1,0:T(8,128)(2,1)S(1)}, u32[]{:S(2)}) copy-start(bf16[30,128,128]{2,1,0:T(8,128)(2,1)S(1)} %collective-permute-done.2.refs_3_) | copy-start | bytes 2949124
  153.1 25.6 %collective-permute-start.5 = (bf16[30,128,128]{2,1,0:T(8,128)(2,1)S(1)}, bf16[30,128,128]{2,1,0:T(8,128)(2,1)S(1)}, u32[]{:S(2)}, u32[]{:S(2)}) collective-permute-start(bf16[30,128,128]{2,1,0:T(8,128)(2,1)S(1)} %collective-permute-done.2.refs_3_), channel_id=1, source_target_pairs={{0,7},{1,6},{2,5},{3,4},{4,3},{5,2},{6,1},{7,0},{8,15},{9,14},{10,... | collective-permute-start | bytes 2949128 | tf_op jit(solution)/shard_map/ppermute | solution.py:238
  155.7 91.1 %copy-start.4 = (bf16[30,128,128]{2,1,0:T(8,128)(2,1)}, bf16[30,128,128]{2,1,0:T(8,128)(2,1)S(1)}, u32[]{:S(2)}) copy-start(bf16[30,128,128]{2,1,0:T(8,128)(2,1)S(1)} %collective-permute-done.3.refs_8_) | copy-start | bytes 2949124
  155.7 24.4 %collective-permute-start.4 = (bf16[30,128,128]{2,1,0:T(8,128)(2,1)S(1)}, bf16[30,128,128]{2,1,0:T(8,128)(2,1)}, u32[]{:S(2)}, u32[]{:S(2)}) collective-permute-start(bf16[30,128,128]{2,1,0:T(8,128)(2,1)S(1)} %collective-permute-done.3.refs_8_), channel_id=1, source_target_pairs={{0,3},{1,2},{2,1},{3,0},{4,7},{5,6},{6,5},{7,4},{8,11},{9,10},{10,... | collective-permute-start | bytes 2949128 | tf_op jit(solution)/shard_map/ppermute | solution.py:238
  155.7 43.1 %collective-permute-start.8 = (bf16[30,128,128]{2,1,0:T(8,128)(2,1)S(1)}, bf16[30,128,128]{2,1,0:T(8,128)(2,1)S(1)}, u32[]{:S(2)}, u32[]{:S(2)}) collective-permute-start(bf16[30,128,128]{2,1,0:T(8,128)(2,1)S(1)} %get-tuple-element.9), channel_id=1, source_target_pairs={{0,7},{1,6},{2,5},{3,4},{4,3},{5,2},{6,1},{7,0},{8,15},{9,14},{10,... | collective-permute-start | bytes 2949128 | tf_op jit(solution)/shard_map/ppermute | solution.py:238
  157.8 42.4 %collective-permute-start.1 = (bf16[30,128,128]{2,1,0:T(8,128)(2,1)S(1)}, bf16[30,128,128]{2,1,0:T(8,128)(2,1)S(1)}, u32[]{:S(2)}, u32[]{:S(2)}) collective-permute-start(bf16[30,128,128]{2,1,0:T(8,128)(2,1)S(1)} %get-tuple-element.10), channel_id=1, source_target_pairs={{0,3},{1,2},{2,1},{3,0},{4,7},{5,6},{6,5},{7,4},{8,11},{9,10},{10,... | collective-permute-start | bytes 2949128 | tf_op jit(solution)/shard_map/ppermute | solution.py:238
  157.9 93.8 %collective-permute-start = (bf16[60,128,128]{2,1,0:T(8,128)(2,1)S(1)}, bf16[60,128,128]{2,1,0:T(8,128)(2,1)}, u32[]{:S(2)}, u32[]{:S(2)}) collective-permute-start(bf16[60,128,128]{2,1,0:T(8,128)(2,1)S(1)} %copy-done), channel_id=1, source_target_pairs={{0,1},{1,0},{2,3},{3,2},{4,5},{5,4},{6,7},{7,6},{8,9},{9,8},{10,11... | collective-permute-start | bytes 5898248 | tf_op jit(solution)/shard_map/ppermute | solution.py:238
  178.6 74.8 %copy-start.1 = (bf16[30,128,128]{2,1,0:T(8,128)(2,1)}, bf16[30,128,128]{2,1,0:T(8,128)(2,1)S(1)}, u32[]{:S(2)}) copy-start(bf16[30,128,128]{2,1,0:T(8,128)(2,1)S(1)} %collective-permute-done.5.refs_5_) | copy-start | bytes 2949124
  178.6 68.2 %collective-permute-start.13 = (bf16[30,128,128]{2,1,0:T(8,128)(2,1)S(1)}, bf16[30,128,128]{2,1,0:T(8,128)(2,1)S(1)}, u32[]{:S(2)}, u32[]{:S(2)}) collective-permute-start(bf16[30,128,128]{2,1,0:T(8,128)(2,1)S(1)} %collective-permute-done.3.refs_8_), channel_id=1, source_target_pairs={{0,8},{1,9},{2,10},{3,11},{4,124},{5,125},{6,126},{7,127},{8,16},{... | collective-permute-start | bytes 2949128 | tf_op jit(solution)/shard_map/ppermute | solution.py:238
  180.1 67.7 %collective-permute-start.9 = (bf16[30,128,128]{2,1,0:T(8,128)(2,1)}, bf16[30,128,128]{2,1,0:T(8,128)(2,1)}, u32[]{:S(2)}, u32[]{:S(2)}) collective-permute-start(bf16[30,128,128]{2,1,0:T(8,128)(2,1)} %collective-permute-done.4.refs_4_), channel_id=1, source_target_pairs={{0,8},{1,9},{2,10},{3,11},{4,124},{5,125},{6,126},{7,127},{8,16},{... | collective-permute-start | bytes 2949128 | tf_op jit(solution)/shard_map/ppermute | solution.py:238
  198.9 2.5 copy-start.2
  198.9 49.4 %collective-permute-start.10 = (bf16[24,128,128]{2,1,0:T(8,128)(2,1)S(1)}, bf16[24,128,128]{2,1,0:T(8,128)(2,1)}, u32[]{:S(2)}, u32[]{:S(2)}) collective-permute-start(bf16[24,128,128]{2,1,0:T(8,128)(2,1)S(1)} %slice.27), channel_id=1, source_target_pairs={{0,8},{1,9},{2,10},{3,11},{4,124},{5,125},{6,126},{7,127},{8,16},{... | collective-permute-start | bytes 2359304 | tf_op jit(solution)/shard_map/ppermute | solution.py:238
  200.1 46.7 %copy-start.5 = (bf16[30,128,128]{2,1,0:T(8,128)(2,1)}, bf16[30,128,128]{2,1,0:T(8,128)(2,1)S(1)}, u32[]{:S(2)}) copy-start(bf16[30,128,128]{2,1,0:T(8,128)(2,1)S(1)} %collective-permute-done.1.refs_2_) | copy-start | bytes 2949124
  200.1 46.6 %collective-permute-start.14 = (bf16[6,128,128]{2,1,0:T(8,128)(2,1)S(1)}, bf16[6,128,128]{2,1,0:T(8,128)(2,1)S(1)}, u32[]{:S(2)}, u32[]{:S(2)}) collective-permute-start(bf16[6,128,128]{2,1,0:T(8,128)(2,1)S(1)} %slice.28), channel_id=1, source_target_pairs={{0,8},{1,9},{2,10},{3,11},{4,124},{5,125},{6,126},{7,127},{8,16},{... | collective-permute-start | bytes 589832 | tf_op jit(solution)/shard_map/ppermute | solution.py:238
  246.8 6.6 %copy-start.7 = (bf16[6,128,128]{2,1,0:T(8,128)(2,1)}, bf16[6,128,128]{2,1,0:T(8,128)(2,1)S(1)}, u32[]{:S(2)}) copy-start(bf16[6,128,128]{2,1,0:T(8,128)(2,1)S(1)} %collective-permute-done.14.refs_15_) | copy-start | bytes 589828
  246.8 4.9 %collective-permute-start.7 = (bf16[30,128,128]{2,1,0:T(8,128)(2,1)S(1)}, bf16[30,128,128]{2,1,0:T(8,128)(2,1)}, u32[]{:S(2)}, u32[]{:S(2)}) collective-permute-start(bf16[30,128,128]{2,1,0:T(8,128)(2,1)S(1)} %collective-permute-done.5.refs_5_), channel_id=1, source_target_pairs={{0,1},{1,0},{2,3},{3,2},{4,5},{5,4},{6,7},{7,6},{8,9},{9,8},{10,11... | collective-permute-start | bytes 2949128 | tf_op jit(solution)/shard_map/ppermute | solution.py:238
  246.8 1.0 copy-start.6
  246.8 4.8 %collective-permute-start.6 = (bf16[30,128,128]{2,1,0:T(8,128)(2,1)}, bf16[30,128,128]{2,1,0:T(8,128)(2,1)}, u32[]{:S(2)}, u32[]{:S(2)}) collective-permute-start(bf16[30,128,128]{2,1,0:T(8,128)(2,1)} %collective-permute-done.4.refs_4_), channel_id=1, source_target_pairs={{0,1},{1,0},{2,3},{3,2},{4,5},{5,4},{6,7},{7,6},{8,9},{9,8},{10,11... | collective-permute-start | bytes 2949128 | tf_op jit(solution)/shard_map/ppermute | solution.py:238
  247.8 5.6 %collective-permute-start.11 = (bf16[30,128,128]{2,1,0:T(8,128)(2,1)}, bf16[30,128,128]{2,1,0:T(8,128)(2,1)}, u32[]{:S(2)}, u32[]{:S(2)}) collective-permute-start(bf16[30,128,128]{2,1,0:T(8,128)(2,1)} %collective-permute-done.9.refs_10_), channel_id=1, source_target_pairs={{0,1},{1,0},{2,3},{3,2},{4,5},{5,4},{6,7},{7,6},{8,9},{9,8},{10,11... | collective-permute-start | bytes 2949128 | tf_op jit(solution)/shard_map/ppermute | solution.py:238
  248.3 5.2 %collective-permute-start.12 = (bf16[24,128,128]{2,1,0:T(8,128)(2,1)}, bf16[24,128,128]{2,1,0:T(8,128)(2,1)}, u32[]{:S(2)}, u32[]{:S(2)}) collective-permute-start(bf16[24,128,128]{2,1,0:T(8,128)(2,1)} %collective-permute-done.10.refs_11_), channel_id=1, source_target_pairs={{0,1},{1,0},{2,3},{3,2},{4,5},{5,4},{6,7},{7,6},{8,9},{9,8},{10,11... | collective-permute-start | bytes 2359304 | tf_op jit(solution)/shard_map/ppermute | solution.py:238
where the time goes:
time: 280 us
  waiting for transfers between devices  202 us (72%)
  Pallas kernels  36.8 us (13%)
  starting transfers between devices  27 us (10%)
  other arithmetic  6.9 us (2%)
  local copies, waits for them, and re-layouts  6.78 us (2%)
    ppermute x15, waiting for transfers between devices, send(): return lax.ppermute(array, axes, pairs)  109 us
    all_to_all x1, waiting for transfers between devices, per_device(): lax.all_to_all(outgoing.reshape(device_count, C, width, width), ('gx', 'g...  92.6 us
    pallas_call x1, Pallas kernels, purify(): pl.pallas_call(functools.partial(purify_kernel, row_count, slot_count, wi...  26 us
    ppermute x15, starting transfers between devices, send(): return lax.ppermute(array, axes, pairs)  15 us
    all_to_all x1, starting transfers between devices, per_device(): lax.all_to_all(outgoing.reshape(device_count, C, width, width), ('gx', 'g...  12 us
    pallas_call x1, Pallas kernels, admit(): pl.pallas_call(admit_kernel, out_shape=jax.ShapeDtypeStruct(density.shape...  7.31 us
  transfers between devices with their start and end apart: 16, of which 7 were waited for; matrix products, arithmetic and copies ran while one was open for 4% of the time, Pallas kernels for 0%

commit v1 on v0

v1 whole, which is shorter than its diff:
```python
import functools

import jax
import jax.numpy as jnp
from jax import lax
from jax.experimental import pallas as pl
from jax.experimental.pallas import tpu as pltpu
from jax.sharding import PartitionSpec as P

C = 2


def pack_kernel(slots_ref, ent_ref, out_ref, staged, load_sems, store_sem):
    count = ent_ref.shape[0]
    parts = load_sems.shape[0]
    size = count // parts
    loads = []
    for p in range(parts):
        rows = pl.ds(p * size, size)
        loads.append(pltpu.make_async_copy(ent_ref.at[rows], staged.at[rows], load_sems.at[p]))
        loads[-1].start()

    def issue(i, carry):
        pltpu.make_async_copy(staged.at[i], out_ref.at[slots_ref[i]], store_sem).start()
        return carry

    for p in range(parts):
        loads[p].wait()
        lax.fori_loop(p * size, (p + 1) * size, issue, 0)
    pltpu.make_async_copy(staged, out_ref.at[pl.ds(0, count)], store_sem).wait()


def pack(ent_blocks, slots, total):
    return pl.pallas_call(
        pack_kernel,
        out_shape=jax.ShapeDtypeStruct((total,) + ent_blocks.shape[1:], ent_blocks.dtype),
        in_specs=[
            pl.BlockSpec(memory_space=pltpu.SMEM),
            pl.BlockSpec(memory_space=pl.ANY),
        ],
        out_specs=pl.BlockSpec(memory_space=pl.ANY),
        scratch_shapes=[
            pltpu.VMEM(ent_blocks.shape, ent_blocks.dtype),
            pltpu.SemaphoreType.DMA((4,)),
            pltpu.SemaphoreType.DMA,
        ],
        name="pack",
    )(slots, ent_blocks)


def admit_kernel(spans, first_ref, order_ref, source_ref, density_ref, received_ref, own_ref, *part_refs):
    def add(j, total):
        return total + received_ref[order_ref[j]].astype(jnp.float32)

    def place(p, carry):
        t = source_ref[p]
        total = lax.fori_loop(
            first_ref[t], first_ref[t + 1], add, density_ref[t].astype(jnp.float32)
        )
        own_ref[p] = total.astype(own_ref.dtype)
        return carry

    lax.fori_loop(0, own_ref.shape[0], place, 0)
    for (low, high), part_ref in zip(spans, part_refs):
        part_ref[...] = own_ref[low:high]


def admit(density, received, first, order, source, spans):
    shapes = [density.shape[0]] + [high - low for low, high in spans]
    return pl.pallas_call(
        functools.partial(admit_kernel, spans),
        out_shape=[
            jax.ShapeDtypeStruct((n,) + density.shape[1:], density.dtype) for n in shapes
        ],
        in_specs=[pl.BlockSpec(memory_space=pltpu.SMEM)] * 3
        + [pl.BlockSpec(memory_space=pltpu.VMEM)] * 2,
        out_specs=[pl.BlockSpec(memory_space=pltpu.VMEM)] * len(shapes),
        name="admit",
    )(first, order, source, density, received)


def reach(part):
    wide, narrow = divmod(part, 3)
    wides = (0, 1, 2) if wide == 0 else (0, wide)
    narrows = (0, 1, 2) if narrow == 0 else (0, narrow)
    return [w * 3 + n for w in wides for n in narrows]


def purify_kernel(row_count, width, piece_starts, zero_at, pos_ref, slot_ref, *refs):
    pieces = refs[: len(piece_starts)]
    out_ref, table, left, grid, square, square_b, staged, sems, out_sem = refs[len(piece_starts):]
    near = 9 * row_count
    group = row_count * width
    copies = []
    for i, (piece, start) in enumerate(zip(pieces, piece_starts)):
        copy = pltpu.make_async_copy(piece, table.at[pl.ds(start, piece.shape[0])], sems.at[i])
        copy.start()
        copies.append(copy)
    table[zero_at] = jnp.zeros((width, width), table.dtype)
    for copy in copies:
        copy.wait()

    for r in range(row_count):
        for k in range(near):
            left[r * width:(r + 1) * width, k * width:(k + 1) * width] = table[
                pos_ref[r * near + k]
            ]

    def lanes_of(ref, parts):
        return jnp.concatenate([ref[:, q * group:(q + 1) * group] for q in parts], axis=1)

    for part in range(9):
        parts = reach(part)
        for i, q in enumerate(parts):
            for r in range(row_count):
                for k in range(row_count):
                    low = (i * row_count + r) * width
                    grid[part, low:low + width, k * width:(k + 1) * width] = table[
                        pos_ref[(q * row_count + r) * near + part * row_count + k]
                    ]
        product = jnp.dot(
            lanes_of(left, parts), grid[part, :len(parts) * group],
            preferred_element_type=jnp.float32,
        )
        lanes = slice(part * group, (part + 1) * group)
        square[:, lanes] = product
        for r in range(row_count):
            for k in range(row_count):
                listed = pos_ref[r * near + part * row_count + k] != zero_at
                low = part * group + k * width
                square_b[r * width:(r + 1) * width, low:low + width] = jnp.where(
                    listed, product[r * width:(r + 1) * width, k * width:(k + 1) * width], 0.0
                ).astype(jnp.bfloat16)

    for part in range(9):
        parts = reach(part)
        product = jnp.dot(
            lanes_of(square_b, parts), grid[part, :len(parts) * group],
            preferred_element_type=jnp.float32,
        )
        result = 3.0 * square[:, part * group:(part + 1) * group] - 2.0 * product
        for r in range(row_count):
            for k in range(row_count):
                staged[slot_ref[r * near + part * row_count + k]] = result[
                    r * width:(r + 1) * width, k * width:(k + 1) * width
                ]
    copy = pltpu.make_async_copy(staged.at[pl.ds(0, out_ref.shape[0])], out_ref, out_sem)
    copy.start()
    copy.wait()


def purify(positions, out_slots, pieces, piece_starts, zero_at, row_count, slot_count, width):
    span = 9 * row_count * width
    group = row_count * width
    blocks = row_count * slot_count
    return pl.pallas_call(
        functools.partial(purify_kernel, row_count, width, piece_starts, zero_at),
        out_shape=jax.ShapeDtypeStruct((blocks, width, width), jnp.float32),
        in_specs=[pl.BlockSpec(memory_space=pltpu.SMEM)] * 2
        + [pl.BlockSpec(memory_space=pl.ANY)] * len(pieces),
        out_specs=pl.BlockSpec(memory_space=pl.ANY),
        scratch_shapes=[
            pltpu.VMEM((zero_at + 1, width, width), jnp.bfloat16),
            pltpu.VMEM((group, span), jnp.bfloat16),
            pltpu.VMEM((9, span, group), jnp.bfloat16),
            pltpu.VMEM((group, span), jnp.float32),
            pltpu.VMEM((group, span), jnp.bfloat16),
            pltpu.VMEM((blocks + 1, width, width), jnp.float32),
            pltpu.SemaphoreType.DMA((len(pieces),)),
            pltpu.SemaphoreType.DMA,
        ],
        name="purify",
    )(positions, out_slots, *pieces)


def block_positions(neighbours, here_x, here_y, starts, zero_at):
    wide_count, narrow_count, row_count, slot_count = neighbours.shape
    total_rows = wide_count * narrow_count * row_count
    listing = neighbours.reshape(total_rows, slot_count)
    ids = jnp.arange(9 * row_count, dtype=jnp.int32)
    wide, narrow, inner = ids // (3 * row_count), ids // row_count % 3, ids % row_count
    beyond = jnp.where(here_x % 2 == 0, here_x + wide_count - 1, here_x + 1) % wide_count
    near_x = jnp.where(wide == 0, here_x, jnp.where(wide == 1, here_x ^ 1, beyond))
    near_y = jnp.where(
        narrow == 0, here_y, jnp.where(narrow == 1, here_y ^ 1, narrow_count - 1 - here_y)
    )
    rows = (near_x * narrow_count + near_y) * row_count + inner
    lists = jnp.take(listing, rows, axis=0)
    list_x = lists // (narrow_count * row_count)
    list_y = lists // row_count % narrow_count
    kind = jnp.where(
        list_x == (near_x ^ 1)[:, None], 2, jnp.where(list_y == (near_y ^ 1)[:, None], 1, 0)
    )
    slot_ids = jnp.arange(slot_count, dtype=jnp.int32)
    key = kind * slot_count + slot_ids
    place = jnp.sum((key[:, :, None] > key[:, None, :]).astype(jnp.int32), axis=2)
    part = wide * 3 + narrow
    start = jnp.zeros_like(part)
    for i, value in enumerate(starts):
        start = jnp.where(part == i, value, start)
    held_at = (start + inner)[:, None] + place * row_count
    matches = lists[:, None, :] == rows[None, :, None]
    positions = jnp.min(jnp.where(matches, held_at[:, None, :], zero_at), axis=2)
    own_matches = matches[:row_count]
    own_slots = slot_ids + slot_count * jnp.arange(row_count, dtype=jnp.int32)[:, None, None]
    out_slots = jnp.min(jnp.where(own_matches, own_slots, row_count * slot_count), axis=2)
    order = (place[:row_count] * row_count + inner[:row_count, None]).reshape(-1)
    flat_ids = jnp.arange(row_count * slot_count, dtype=jnp.int32)
    source = jnp.sum(jnp.where(order[None, :] == flat_ids[:, None], flat_ids[None, :], 0), axis=1)
    return (
        positions.astype(jnp.int32).reshape(-1),
        out_slots.astype(jnp.int32).reshape(-1),
        source.astype(jnp.int32),
    )


def per_device(density, neighbours, ent_blocks, ent_owner, ent_place):
    wide_count = lax.axis_size("gx")
    narrow_count = lax.axis_size("gy")
    device_count = wide_count * narrow_count
    here_x = lax.axis_index("gx")
    here_y = lax.axis_index("gy")
    self_index = here_x * narrow_count + here_y
    row_count = density.shape[2]
    slot_count = density.shape[3]
    width = density.shape[4]
    blocks = row_count * slot_count
    held = ent_blocks.shape[0]
    owners = ent_owner.reshape(device_count, held)
    places = ent_place.reshape(device_count, held)

    my_owners = lax.dynamic_index_in_dim(owners, self_index, 0, False)
    entry_ids = jnp.arange(held, dtype=jnp.int32)
    same = my_owners[:, None] == my_owners[None, :]
    my_ranks = jnp.sum(same & (entry_ids[None, :] < entry_ids[:, None]), axis=1)
    slots = (my_owners * C + my_ranks).astype(jnp.int32)
    outgoing = pack(ent_blocks, slots, device_count * C)
    received = lax.all_to_all(
        outgoing.reshape(device_count, C, width, width),
        ("gx", "gy"), split_axis=0, concat_axis=0, tiled=True,
    ).reshape(device_count * C, width, width)

    for_me = (owners == self_index).astype(jnp.int32)
    rank = jnp.cumsum(for_me, axis=1) - for_me
    picked = (for_me[:, :, None] == 1) & (
        rank[:, :, None] == jnp.arange(C, dtype=jnp.int32)[None, None, :]
    )
    slot_place = jnp.sum(jnp.where(picked, places[:, :, None], 0), axis=1).reshape(-1)
    slot_used = jnp.any(picked, axis=1).reshape(-1)
    slot_place = jnp.where(slot_used, slot_place, blocks)
    slot_ids = jnp.arange(device_count * C, dtype=jnp.int32)
    ahead = (slot_place[:, None] > slot_place[None, :]) | (
        (slot_place[:, None] == slot_place[None, :]) & (slot_ids[:, None] > slot_ids[None, :])
    )
    sorted_at = jnp.sum(ahead, axis=1)
    order = jnp.sum(
        jnp.where(sorted_at[None, :] == slot_ids[:, None], slot_ids[None, :], 0), axis=1
    ).astype(jnp.int32)
    target_ids = jnp.arange(blocks + 1, dtype=jnp.int32)
    first = jnp.sum(slot_place[None, :] < target_ids[:, None], axis=1).astype(jnp.int32)

    near_blocks = row_count * min(slot_count, 6 * row_count)
    corner_blocks = row_count * min(slot_count, 4 * row_count)
    sizes = [blocks] * 6 + [near_blocks, near_blocks, corner_blocks]
    starts = [sum(sizes[:i]) for i in range(9)]
    zero_at = sum(sizes)
    positions, out_slots, source = block_positions(neighbours, here_x, here_y, starts, zero_at)

    cut = corner_blocks // 2
    spans = ((0, cut), (cut, 2 * cut), (2 * cut, blocks), (0, 2 * cut))
    own, own_1, own_2, own_3, own_12 = admit(
        density.reshape(blocks, width, width), received, first, order, source, spans
    )

    axes = ("gx", "gy")
    devices = [(x, y) for x in range(wide_count) for y in range(narrow_count)]

    def send(array, target):
        pairs = []
        for x, y in devices:
            to_x, to_y = target(x, y)
            pairs.append((x * narrow_count + y, to_x % wide_count * narrow_count + to_y))
        return lax.ppermute(array, axes, pairs)

    def across(x, y):
        return x, narrow_count - 1 - y

    def chip(x, y):
        return x, y ^ 1

    def ring(x, y):
        return x ^ 1, narrow_count - 1 - y

    def onward(x, y):
        return (x + 2 if x % 2 == 0 else x - 2), y

    ring_across_1 = send(own_1, ring)
    own_across_3 = send(own_3, across)
    ring_across_2 = send(own_2, ring)
    own_chip = send(own, chip)
    far_across_1 = send(ring_across_1, onward)
    ring_same_1 = send(ring_across_1, across)
    ring_same_3 = send(own_across_3, ring)
    far_across_2 = send(ring_across_2, onward)
    ring_same_2 = send(ring_across_2, across)
    ring_across_3 = send(own_3, ring)
    own_across_12 = send(own_12, across)
    far_same_1 = send(ring_same_1, onward)
    ring_chip_1 = send(ring_same_1, chip)
    far_same_2 = send(ring_same_2, onward)
    ring_chip_2 = send(ring_same_2, chip)
    far_same_3 = send(ring_same_3[:near_blocks - 2 * cut], onward)
    ring_chip_3 = send(ring_same_3, chip)
    far_chip_1 = send(far_same_1, chip)
    far_chip_2 = send(far_same_2, chip)
    far_chip_3 = send(far_same_3, chip)

    pieces = [
        (own, 0, 0), (own_chip, 1, 0), (own_across_12, 2, 0), (own_across_3, 2, 2 * cut),
        (ring_same_1, 3, 0), (ring_same_2, 3, cut), (ring_same_3, 3, 2 * cut),
        (ring_chip_1, 4, 0), (ring_chip_2, 4, cut), (ring_chip_3, 4, 2 * cut),
        (ring_across_1, 5, 0), (ring_across_2, 5, cut), (ring_across_3, 5, 2 * cut),
        (far_same_1, 6, 0), (far_same_2, 6, cut), (far_same_3, 6, 2 * cut),
        (far_chip_1, 7, 0), (far_chip_2, 7, cut), (far_chip_3, 7, 2 * cut),
        (far_across_1, 8, 0), (far_across_2, 8, cut),
    ]
    purified = purify(
        positions, out_slots, [piece for piece, _, _ in pieces],
        [starts[part] + offset for _, part, offset in pieces],
        zero_at, row_count, slot_count, width,
    )
    return purified.reshape(density.shape)


def solution(mesh):
    in_specs = (P("gx", "gy", None, None, None, None), P(), P(("gx", "gy"), None, None), P(), P())
    out_specs = P("gx", "gy", None, None, None, None)
    return jax.shard_map(
        per_device, mesh=mesh, in_specs=in_specs, out_specs=out_specs, check_vma=False
    )
```

time: 280 us -> 265 us (0.946)
  waiting for transfers between devices: 202 us -> 175 us
  starting transfers between devices: 27 us -> 33 us
  local copies, waits for them, and re-layouts: 6.78 us -> 10.7 us
    ppermute x15 -> x20, waiting for transfers between devices: 109 us -> 81.3 us  [send(): return lax.ppermute(array, axes, pairs)]
    ppermute x15 -> x20, starting transfers between devices: 15 us -> 21.1 us  [send(): return lax.ppermute(array, axes, pairs)]
  transfers between devices with their start and end apart: 16 -> 21, of which waited for: 7 -> 11; matrix products, arithmetic and copies ran while one was open for 4% -> 6% of each run, Pallas kernels for 0% -> 0%
where the time goes in v1:
time: 265 us; the launch traced here: 264 us
  waiting for transfers between devices  175 us (66%)
  Pallas kernels  36.2 us (14%)
  starting transfers between devices  33 us (12%)
  local copies, waits for them, and re-layouts  10.7 us (4%)
  other arithmetic  8.78 us (3%)
    all_to_all x1, waiting for transfers between devices, per_device(): lax.all_to_all(outgoing.reshape(device_count, C, width, width), ('gx', 'g...  93.8 us
    ppermute x20, waiting for transfers between devices, send(): return lax.ppermute(array, axes, pairs)  81.3 us
    pallas_call x1, Pallas kernels, purify(): pl.pallas_call(functools.partial(purify_kernel, row_count, width, piece_s...  24.3 us
    ppermute x20, starting transfers between devices, send(): return lax.ppermute(array, axes, pairs)  21.1 us
    all_to_all x1, starting transfers between devices, per_device(): lax.all_to_all(outgoing.reshape(device_count, C, width, width), ('gx', 'g...  11.9 us
    pallas_call x1, Pallas kernels, admit(): pl.pallas_call(functools.partial(admit_kernel, spans), out_shape=[jax.Sha...  8.47 us
  transfers between devices with their start and end apart: 21, of which 11 were waited for; matrix products, arithmetic and copies ran while one was open for 6% of the time, Pallas kernels for 0%

profile of v1, /device:TPU:1, one launch (start us, length us, event | category | flops | bytes accessed | tf_op | source)
XLA Modules:
  0.0 264.3 jit_solution(10947179758708586100)
XLA Ops:
  0.0 0.9 reshape.489
  1.6 3.5 %pack.1 = bf16[256,128,128]{2,1,0:T(8,128)(2,1)} custom-call(s32[96]{0:T(128)} %multiply_add_fusion.2.slots_ref, bf16[96,128,128]{2,1,0:T(8,128)(2,1)} %ent_ref.1), custom_call_target="tpu_custom_call" | custom-call | tf_op jit(solution)/shard_map/pack/pallas_call | solution.py:34
  5.1 11.9 %all-to-all-start = ((bf16[128,2,128,128]{3,2,1,0:T(8,128)(2,1)}), bf16[128,2,128,128]{3,2,1,0:T(8,128)(2,1)}, u32[]{:S(2)}, u32[]{:S(2)}) async-start(bf16[128,2,128,128]{3,2,1,0:T(8,128)(2,1)} %bitcast.12), calls=%async_computation | async-start | bytes 16777216 | tf_op jit(solution)/shard_map/all_to_all | solution.py:238
  22.6 93.8 %all-to-all-done = bf16[128,2,128,128]{3,2,1,0:T(8,128)(2,1)} async-done(((bf16[128,2,128,128]{3,2,1,0:T(8,128)(2,1)}), bf16[128,2,128,128]{3,2,1,0:T(8,128)(2,1)}, u32[]{:S(2)}, u32[]{:S(2)}) %all-to-all-start) | async-done | bytes 8388640 | tf_op jit(solution)/shard_map/all_to_all | solution.py:238
  116.4 8.5 %admit.1 = (bf16[60,128,128]{2,1,0:T(8,128)(2,1)}, bf16[18,128,128]{2,1,0:T(8,128)(2,1)}, bf16[18,128,128]{2,1,0:T(8,128)(2,1)}, bf16[24,128,128]{2,1,0:T(8,128)(2,1)}, bf16[36,128,128]{2,1,0:T(8,128)(2,1)}) custom-call(s32[61]{0:T(128)} %convert_reduce_fusion.2.first_ref, s32[256]{0:T(256)} %select_reduce_fusion.1.order_ref, ...), custom_call_target="tpu_custom_call" | custom-call | tf_op jit(solution)/shard_map/admit/pallas_call | solution.py:70
  124.9 6.1 %collective-permute-start.1 = (bf16[36,128,128]{2,1,0:T(8,128)(2,1)}, bf16[36,128,128]{2,1,0:T(8,128)(2,1)S(1)}, u32[]{:S(2)}, u32[]{:S(2)}) collective-permute-start(bf16[36,128,128]{2,1,0:T(8,128)(2,1)} %get-tuple-element.11), channel_id=1, source_target_pairs={{0,3},{1,2},{2,1},{3,0},{4,7},{5,6},{6,5},{7,4},{8,11},{9,10},{10,... | collective-permute-start | bytes 3538952 | tf_op jit(solution)/shard_map/ppermute | solution.py:283
  131.0 3.0 %collective-permute-start.5 = (bf16[18,128,128]{2,1,0:T(8,128)(2,1)}, bf16[18,128,128]{2,1,0:T(8,128)(2,1)S(1)}, u32[]{:S(2)}, u32[]{:S(2)}) collective-permute-start(bf16[18,128,128]{2,1,0:T(8,128)(2,1)} %get-tuple-element.14), channel_id=1, source_target_pairs={{0,7},{1,6},{2,5},{3,4},{4,3},{5,2},{6,1},{7,0},{8,15},{9,14},{10,... | collective-permute-start | bytes 1769480 | tf_op jit(solution)/shard_map/ppermute | solution.py:283
  134.0 14.3 %collective-permute-done.3.refs_10_ = bf16[18,128,128]{2,1,0:T(8,128)(2,1)S(1)} collective-permute-done((bf16[18,128,128]{2,1,0:T(8,128)(2,1)}, bf16[18,128,128]{2,1,0:T(8,128)(2,1)S(1)}, u32[]{:S(2)}, u32[]{:S(2)}) %collective-permute-start.3) | collective-permute-done | bytes 589856 | tf_op jit(solution)/shard_map/ppermute | solution.py:283
  148.3 1.5 collective-permute-start.18
  149.8 11.2 %collective-permute-done.5.refs_11_ = bf16[18,128,128]{2,1,0:T(8,128)(2,1)S(1)} collective-permute-done((bf16[18,128,128]{2,1,0:T(8,128)(2,1)}, bf16[18,128,128]{2,1,0:T(8,128)(2,1)S(1)}, u32[]{:S(2)}, u32[]{:S(2)}) %collective-permute-start.5) | collective-permute-done | bytes 589856 | tf_op jit(solution)/shard_map/ppermute | solution.py:283
  160.9 14.0 %collective-permute-done.2.refs_3_ = bf16[24,128,128]{2,1,0:T(8,128)(2,1)S(1)} collective-permute-done((bf16[24,128,128]{2,1,0:T(8,128)(2,1)}, bf16[24,128,128]{2,1,0:T(8,128)(2,1)S(1)}, u32[]{:S(2)}, u32[]{:S(2)}) %collective-permute-start.2) | collective-permute-done | bytes 786464 | tf_op jit(solution)/shard_map/ppermute | solution.py:283
  174.9 1.3 collective-permute-done.11.refs_12_
  176.3 0.9 copy-done.4
  177.3 1.7 collective-permute-start.19
  179.0 8.6 %collective-permute-done.4.refs_4_ = bf16[18,128,128]{2,1,0:T(8,128)(2,1)} collective-permute-done((bf16[18,128,128]{2,1,0:T(8,128)(2,1)S(1)}, bf16[18,128,128]{2,1,0:T(8,128)(2,1)}, u32[]{:S(2)}, u32[]{:S(2)}) %collective-permute-start.4) | collective-permute-done | bytes 589856 | tf_op jit(solution)/shard_map/ppermute | solution.py:283
  187.6 1.5 collective-permute-start.12
  189.0 5.2 %collective-permute-done.7.refs_6_ = bf16[24,128,128]{2,1,0:T(8,128)(2,1)S(1)} collective-permute-done((bf16[24,128,128]{2,1,0:T(8,128)(2,1)S(1)}, bf16[24,128,128]{2,1,0:T(8,128)(2,1)S(1)}, u32[]{:S(2)}, u32[]{:S(2)}) %collective-permute-start.7) | collective-permute-done | bytes 786464 | tf_op jit(solution)/shard_map/ppermute | solution.py:283
  194.4 1.0 slice.20
  195.3 3.7 %collective-permute-done.6.refs_5_ = bf16[18,128,128]{2,1,0:T(8,128)(2,1)} collective-permute-done((bf16[18,128,128]{2,1,0:T(8,128)(2,1)S(1)}, bf16[18,128,128]{2,1,0:T(8,128)(2,1)}, u32[]{:S(2)}, u32[]{:S(2)}) %collective-permute-start.6) | collective-permute-done | bytes 589856 | tf_op jit(solution)/shard_map/ppermute | solution.py:283
  199.0 1.5 collective-permute-start.13
  200.5 0.8 copy-done.8
  201.4 6.5 %collective-permute-done.12.refs_13_ = bf16[18,128,128]{2,1,0:T(8,128)(2,1)} collective-permute-done((bf16[18,128,128]{2,1,0:T(8,128)(2,1)}, bf16[18,128,128]{2,1,0:T(8,128)(2,1)}, u32[]{:S(2)}, u32[]{:S(2)}) %collective-permute-start.12) | collective-permute-done | bytes 589856 | tf_op jit(solution)/shard_map/ppermute | solution.py:283
  208.5 1.4 copy.25
  210.7 2.2 collective-permute-start.10
  212.9 1.6 select_reduce_fusion
  214.5 6.0 %collective-permute-done.13.refs_14_ = bf16[18,128,128]{2,1,0:T(8,128)(2,1)} collective-permute-done((bf16[18,128,128]{2,1,0:T(8,128)(2,1)}, bf16[18,128,128]{2,1,0:T(8,128)(2,1)}, u32[]{:S(2)}, u32[]{:S(2)}) %collective-permute-start.13) | collective-permute-done | bytes 589856 | tf_op jit(solution)/shard_map/ppermute | solution.py:283
  220.5 2.1 collective-permute-start.15
  222.7 10.5 %collective-permute-done.14.refs_15_ = bf16[18,128,128]{2,1,0:T(8,128)(2,1)} collective-permute-done((bf16[18,128,128]{2,1,0:T(8,128)(2,1)}, bf16[18,128,128]{2,1,0:T(8,128)(2,1)}, u32[]{:S(2)}, u32[]{:S(2)}) %collective-permute-start.14) | collective-permute-done | bytes 589856 | tf_op jit(solution)/shard_map/ppermute | solution.py:283
  233.2 1.3 collective-permute-start.17
  235.0 1.4 reshape.487.pos_ref
  238.7 1.2 copy-done.1
  239.9 24.3 %purify.1 = f32[60,128,128]{2,1,0:T(8,128)} custom-call(s32[729]{0:T(1024)} %reshape.487.pos_ref, s32[81]{0:T(128)} %reshape.488.slot_ref, bf16[60,128,128]{2,1,0:T(8,128)(2,1)} %get-tuple-element.10.refs_0_, bf16[60,128,128]{2,1,0:T(8,128)(2,1)} %copy-done.1, bf16[36,128,128]{2,1,0:T(8,128)(2,1)} %copy-done.2, bf16[24,128,128]{2,1,0:T(8,128)(2,1)} %copy-done.3, ...), custom_call_target="tpu_custom_call" | custom-call | tf_op jit(solution)/shard_map/purify/pallas_call | solution.py:156
  (80 shorter events, 10.7 us)
Async XLA Ops:
  5.1 12.2 %copy-start.10 = (s32[12288]{0:T(1024)S(1)}, s32[12288]{0:T(1024)}, u32[]{:S(2)}) copy-start(s32[12288]{0:T(1024)} %param.9) | copy-start | bytes 147460
  5.1 12.7 %copy-start.9 = (s32[32,4,3,20]{0,1,3,2:T(4,128)S(1)}, s32[32,4,3,20]{0,1,3,2:T(4,128)}, u32[]{:S(2)}) copy-start(s32[32,4,3,20]{0,1,3,2:T(4,128)} %param.6) | copy-start | bytes 92164
  5.1 111.3 %all-to-all-start = ((bf16[128,2,128,128]{3,2,1,0:T(8,128)(2,1)}), bf16[128,2,128,128]{3,2,1,0:T(8,128)(2,1)}, u32[]{:S(2)}, u32[]{:S(2)}) async-start(bf16[128,2,128,128]{3,2,1,0:T(8,128)(2,1)} %bitcast.12), calls=%async_computation | async-start | bytes 16777216 | tf_op jit(solution)/shard_map/all_to_all | solution.py:238
  124.9 52.3 %collective-permute-start.1 = (bf16[36,128,128]{2,1,0:T(8,128)(2,1)}, bf16[36,128,128]{2,1,0:T(8,128)(2,1)S(1)}, u32[]{:S(2)}, u32[]{:S(2)}) collective-permute-start(bf16[36,128,128]{2,1,0:T(8,128)(2,1)} %get-tuple-element.11), channel_id=1, source_target_pairs={{0,3},{1,2},{2,1},{3,0},{4,7},{5,6},{6,5},{7,4},{8,11},{9,10},{10,... | collective-permute-start | bytes 3538952 | tf_op jit(solution)/shard_map/ppermute | solution.py:283
  131.0 17.3 %collective-permute-start.3 = (bf16[18,128,128]{2,1,0:T(8,128)(2,1)}, bf16[18,128,128]{2,1,0:T(8,128)(2,1)S(1)}, u32[]{:S(2)}, u32[]{:S(2)}) collective-permute-start(bf16[18,128,128]{2,1,0:T(8,128)(2,1)} %get-tuple-element.13), channel_id=1, source_target_pairs={{0,7},{1,6},{2,5},{3,4},{4,3},{5,2},{6,1},{7,0},{8,15},{9,14},{10,... | collective-permute-start | bytes 1769480 | tf_op jit(solution)/shard_map/ppermute | solution.py:283
  131.0 30.0 %collective-permute-start.5 = (bf16[18,128,128]{2,1,0:T(8,128)(2,1)}, bf16[18,128,128]{2,1,0:T(8,128)(2,1)S(1)}, u32[]{:S(2)}, u32[]{:S(2)}) collective-permute-start(bf16[18,128,128]{2,1,0:T(8,128)(2,1)} %get-tuple-element.14), channel_id=1, source_target_pairs={{0,7},{1,6},{2,5},{3,4},{4,3},{5,2},{6,1},{7,0},{8,15},{9,14},{10,... | collective-permute-start | bytes 1769480 | tf_op jit(solution)/shard_map/ppermute | solution.py:283
  133.9 41.0 %collective-permute-start.2 = (bf16[24,128,128]{2,1,0:T(8,128)(2,1)}, bf16[24,128,128]{2,1,0:T(8,128)(2,1)S(1)}, u32[]{:S(2)}, u32[]{:S(2)}) collective-permute-start(bf16[24,128,128]{2,1,0:T(8,128)(2,1)} %get-tuple-element.12), channel_id=1, source_target_pairs={{0,3},{1,2},{2,1},{3,0},{4,7},{5,6},{6,5},{7,4},{8,11},{9,10},{10,... | collective-permute-start | bytes 2359304 | tf_op jit(solution)/shard_map/ppermute | solution.py:283
  133.9 42.4 %collective-permute-start.11 = (bf16[24,128,128]{2,1,0:T(8,128)(2,1)}, bf16[24,128,128]{2,1,0:T(8,128)(2,1)S(1)}, u32[]{:S(2)}, u32[]{:S(2)}) collective-permute-start(bf16[24,128,128]{2,1,0:T(8,128)(2,1)} %get-tuple-element.12), channel_id=1, source_target_pairs={{0,7},{1,6},{2,5},{3,4},{4,3},{5,2},{6,1},{7,0},{8,15},{9,14},{10,... | collective-permute-start | bytes 2359304 | tf_op jit(solution)/shard_map/ppermute | solution.py:283
  148.3 46.0 %copy-start.5 = (bf16[18,128,128]{2,1,0:T(8,128)(2,1)}, bf16[18,128,128]{2,1,0:T(8,128)(2,1)S(1)}, u32[]{:S(2)}) copy-start(bf16[18,128,128]{2,1,0:T(8,128)(2,1)S(1)} %collective-permute-done.3.refs_10_) | copy-start | bytes 1769476
  148.3 29.0 %collective-permute-start.18 = (bf16[18,128,128]{2,1,0:T(8,128)(2,1)S(1)}, bf16[18,128,128]{2,1,0:T(8,128)(2,1)S(1)}, u32[]{:S(2)}, u32[]{:S(2)}) collective-permute-start(bf16[18,128,128]{2,1,0:T(8,128)(2,1)S(1)} %collective-permute-done.3.refs_10_), channel_id=1, source_target_pairs={{0,8},{1,9},{2,10},{3,11},{4,124},{5,125},{6,126},{7,127},{8,16},{... | collective-permute-start | bytes 1769480 | tf_op jit(solution)/shard_map/ppermute | solution.py:283
  160.9 33.4 %copy-start.6 = (bf16[18,128,128]{2,1,0:T(8,128)(2,1)}, bf16[18,128,128]{2,1,0:T(8,128)(2,1)S(1)}, u32[]{:S(2)}) copy-start(bf16[18,128,128]{2,1,0:T(8,128)(2,1)S(1)} %collective-permute-done.5.refs_11_) | copy-start | bytes 1769476
  160.9 26.6 %collective-permute-start.4 = (bf16[18,128,128]{2,1,0:T(8,128)(2,1)S(1)}, bf16[18,128,128]{2,1,0:T(8,128)(2,1)}, u32[]{:S(2)}, u32[]{:S(2)}) collective-permute-start(bf16[18,128,128]{2,1,0:T(8,128)(2,1)S(1)} %collective-permute-done.3.refs_10_), channel_id=1, source_target_pairs={{0,3},{1,2},{2,1},{3,0},{4,7},{5,6},{6,5},{7,4},{8,11},{9,10},{10,... | collective-permute-start | bytes 1769480 | tf_op jit(solution)/shard_map/ppermute | solution.py:283
  174.9 63.7 %copy-start.3 = (bf16[24,128,128]{2,1,0:T(8,128)(2,1)}, bf16[24,128,128]{2,1,0:T(8,128)(2,1)S(1)}, u32[]{:S(2)}) copy-start(bf16[24,128,128]{2,1,0:T(8,128)(2,1)S(1)} %collective-permute-done.2.refs_3_) | copy-start | bytes 2359300
  174.9 19.3 %collective-permute-start.7 = (bf16[24,128,128]{2,1,0:T(8,128)(2,1)S(1)}, bf16[24,128,128]{2,1,0:T(8,128)(2,1)S(1)}, u32[]{:S(2)}, u32[]{:S(2)}) collective-permute-start(bf16[24,128,128]{2,1,0:T(8,128)(2,1)S(1)} %collective-permute-done.2.refs_3_), channel_id=1, source_target_pairs={{0,7},{1,6},{2,5},{3,4},{4,3},{5,2},{6,1},{7,0},{8,15},{9,14},{10,... | collective-permute-start | bytes 2359304 | tf_op jit(solution)/shard_map/ppermute | solution.py:283
  176.3 0.9 copy-start.4
  177.2 61.5 %collective-permute-start = (bf16[60,128,128]{2,1,0:T(8,128)(2,1)}, bf16[60,128,128]{2,1,0:T(8,128)(2,1)S(1)}, u32[]{:S(2)}, u32[]{:S(2)}) collective-permute-start(bf16[60,128,128]{2,1,0:T(8,128)(2,1)} %get-tuple-element.10.refs_0_), channel_id=1, source_target_pairs={{0,1},{1,0},{2,3},{3,2},{4,5},{5,4},{6,7},{7,6},{8,9},{9,8},{10,11... | collective-permute-start | bytes 5898248 | tf_op jit(solution)/shard_map/ppermute | solution.py:283
  177.2 17.1 %copy-start.2 = (bf16[36,128,128]{2,1,0:T(8,128)(2,1)}, bf16[36,128,128]{2,1,0:T(8,128)(2,1)S(1)}, u32[]{:S(2)}) copy-start(bf16[36,128,128]{2,1,0:T(8,128)(2,1)S(1)} %collective-permute-done.1.refs_2_) | copy-start | bytes 3538948
  177.2 21.8 %collective-permute-start.6 = (bf16[18,128,128]{2,1,0:T(8,128)(2,1)S(1)}, bf16[18,128,128]{2,1,0:T(8,128)(2,1)}, u32[]{:S(2)}, u32[]{:S(2)}) collective-permute-start(bf16[18,128,128]{2,1,0:T(8,128)(2,1)S(1)} %collective-permute-done.5.refs_11_), channel_id=1, source_target_pairs={{0,3},{1,2},{2,1},{3,0},{4,7},{5,6},{6,5},{7,4},{8,11},{9,10},{10,... | collective-permute-start | bytes 1769480 | tf_op jit(solution)/shard_map/ppermute | solution.py:283
  177.3 16.9 %copy-start.7 = (bf16[18,128,128]{2,1,0:T(8,128)(2,1)}, bf16[18,128,128]{2,1,0:T(8,128)(2,1)S(1)}, u32[]{:S(2)}) copy-start(bf16[18,128,128]{2,1,0:T(8,128)(2,1)S(1)} %collective-permute-done.18.refs_19_) | copy-start | bytes 1769476
  177.3 23.2 %collective-permute-start.19 = (bf16[18,128,128]{2,1,0:T(8,128)(2,1)S(1)}, bf16[18,128,128]{2,1,0:T(8,128)(2,1)S(1)}, u32[]{:S(2)}, u32[]{:S(2)}) collective-permute-start(bf16[18,128,128]{2,1,0:T(8,128)(2,1)S(1)} %collective-permute-done.5.refs_11_), channel_id=1, source_target_pairs={{0,8},{1,9},{2,10},{3,11},{4,124},{5,125},{6,126},{7,127},{8,16},{... | collective-permute-start | bytes 1769480 | tf_op jit(solution)/shard_map/ppermute | solution.py:283
  187.6 20.3 %collective-permute-start.12 = (bf16[18,128,128]{2,1,0:T(8,128)(2,1)}, bf16[18,128,128]{2,1,0:T(8,128)(2,1)}, u32[]{:S(2)}, u32[]{:S(2)}) collective-permute-start(bf16[18,128,128]{2,1,0:T(8,128)(2,1)} %collective-permute-done.4.refs_4_), channel_id=1, source_target_pairs={{0,8},{1,9},{2,10},{3,11},{4,124},{5,125},{6,126},{7,127},{8,16},{... | collective-permute-start | bytes 1769480 | tf_op jit(solution)/shard_map/ppermute | solution.py:283
  194.3 44.4 %copy-start = (bf16[24,128,128]{2,1,0:T(8,128)(2,1)}, bf16[24,128,128]{2,1,0:T(8,128)(2,1)S(1)}, u32[]{:S(2)}) copy-start(bf16[24,128,128]{2,1,0:T(8,128)(2,1)S(1)} %collective-permute-done.7.refs_6_) | copy-start | bytes 2359300
  194.3 16.5 %collective-permute-start.8 = (bf16[18,128,128]{2,1,0:T(8,128)(2,1)}, bf16[18,128,128]{2,1,0:T(8,128)(2,1)}, u32[]{:S(2)}, u32[]{:S(2)}) collective-permute-start(bf16[18,128,128]{2,1,0:T(8,128)(2,1)} %collective-permute-done.4.refs_4_), channel_id=1, source_target_pairs={{0,1},{1,0},{2,3},{3,2},{4,5},{5,4},{6,7},{7,6},{8,9},{9,8},{10,11... | collective-permute-start | bytes 1769480 | tf_op jit(solution)/shard_map/ppermute | solution.py:283
  199.0 21.5 %collective-permute-start.13 = (bf16[18,128,128]{2,1,0:T(8,128)(2,1)}, bf16[18,128,128]{2,1,0:T(8,128)(2,1)}, u32[]{:S(2)}, u32[]{:S(2)}) collective-permute-start(bf16[18,128,128]{2,1,0:T(8,128)(2,1)} %collective-permute-done.6.refs_5_), channel_id=1, source_target_pairs={{0,8},{1,9},{2,10},{3,11},{4,124},{5,125},{6,126},{7,127},{8,16},{... | collective-permute-start | bytes 1769480 | tf_op jit(solution)/shard_map/ppermute | solution.py:283
  200.5 0.8 copy-start.8
  201.3 21.4 %collective-permute-start.9 = (bf16[18,128,128]{2,1,0:T(8,128)(2,1)}, bf16[18,128,128]{2,1,0:T(8,128)(2,1)}, u32[]{:S(2)}, u32[]{:S(2)}) collective-permute-start(bf16[18,128,128]{2,1,0:T(8,128)(2,1)} %collective-permute-done.6.refs_5_), channel_id=1, source_target_pairs={{0,1},{1,0},{2,3},{3,2},{4,5},{5,4},{6,7},{7,6},{8,9},{9,8},{10,11... | collective-permute-start | bytes 1769480 | tf_op jit(solution)/shard_map/ppermute | solution.py:283
  207.9 25.3 %collective-permute-start.14 = (bf16[18,128,128]{2,1,0:T(8,128)(2,1)}, bf16[18,128,128]{2,1,0:T(8,128)(2,1)}, u32[]{:S(2)}, u32[]{:S(2)}) collective-permute-start(bf16[18,128,128]{2,1,0:T(8,128)(2,1)} %slice.20), channel_id=1, source_target_pairs={{0,8},{1,9},{2,10},{3,11},{4,124},{5,125},{6,126},{7,127},{8,16},{... | collective-permute-start | bytes 1769480 | tf_op jit(solution)/shard_map/ppermute | solution.py:283
  210.7 27.9 %collective-permute-start.10 = (bf16[24,128,128]{2,1,0:T(8,128)(2,1)S(1)}, bf16[24,128,128]{2,1,0:T(8,128)(2,1)}, u32[]{:S(2)}, u32[]{:S(2)}) collective-permute-start(bf16[24,128,128]{2,1,0:T(8,128)(2,1)S(1)} %collective-permute-done.7.refs_6_), channel_id=1, source_target_pairs={{0,1},{1,0},{2,3},{3,2},{4,5},{5,4},{6,7},{7,6},{8,9},{9,8},{10,11... | collective-permute-start | bytes 2359304 | tf_op jit(solution)/shard_map/ppermute | solution.py:283
  220.5 18.1 %collective-permute-start.15 = (bf16[18,128,128]{2,1,0:T(8,128)(2,1)}, bf16[18,128,128]{2,1,0:T(8,128)(2,1)}, u32[]{:S(2)}, u32[]{:S(2)}) collective-permute-start(bf16[18,128,128]{2,1,0:T(8,128)(2,1)} %collective-permute-done.12.refs_13_), channel_id=1, source_target_pairs={{0,1},{1,0},{2,3},{3,2},{4,5},{5,4},{6,7},{7,6},{8,9},{9,8},{10,11... | collective-permute-start | bytes 1769480 | tf_op jit(solution)/shard_map/ppermute | solution.py:283
  222.7 15.9 %collective-permute-start.16 = (bf16[18,128,128]{2,1,0:T(8,128)(2,1)}, bf16[18,128,128]{2,1,0:T(8,128)(2,1)}, u32[]{:S(2)}, u32[]{:S(2)}) collective-permute-start(bf16[18,128,128]{2,1,0:T(8,128)(2,1)} %collective-permute-done.13.refs_14_), channel_id=1, source_target_pairs={{0,1},{1,0},{2,3},{3,2},{4,5},{5,4},{6,7},{7,6},{8,9},{9,8},{10,11... | collective-permute-start | bytes 1769480 | tf_op jit(solution)/shard_map/ppermute | solution.py:283
  233.2 5.5 %collective-permute-start.17 = (bf16[18,128,128]{2,1,0:T(8,128)(2,1)}, bf16[18,128,128]{2,1,0:T(8,128)(2,1)}, u32[]{:S(2)}, u32[]{:S(2)}) collective-permute-start(bf16[18,128,128]{2,1,0:T(8,128)(2,1)} %collective-permute-done.14.refs_15_), channel_id=1, source_target_pairs={{0,1},{1,0},{2,3},{3,2},{4,5},{5,4},{6,7},{7,6},{8,9},{9,8},{10,11... | collective-permute-start | bytes 1769480 | tf_op jit(solution)/shard_map/ppermute | solution.py:283
  238.6 1.3 copy-start.1
